TPU v7x, 256 devices: a whole 4x4x8 slice. The times are simulated.
256 devices in a mesh: row: 16 (over z, core), col: 16 (over x, y).
Axes of the slice: x: 4, y: 4, z: 8, core: 2. Of those that a mesh axis runs over, the one named last changes fastest.
Arguments:
- eigvec: float32 [32768, 8192], P('row', 'col'), may hold values from -6 to 6
- slots: float32 [16, 32768, 256], P('col', 'row'), may hold values from -0.03125 to 0.03125
- roots: int32 [3], replicated, may hold values from 0 to 15, as said below
- tfac: float32 [3, 256, 256], replicated, as said below
Outputs:
- transformed: float32 [32768, 8192], P('row', 'col')
Inputs may be any that keep to these rules, and one draw needn't show every extreme that they name: The panels lie in consecutive grid columns, roots[k] = (roots[0] + k) mod 16; roots[0] is one of the last two grid columns, so the panels always wrap past the last grid column. tfac[k] is upper triangular with a diagonal between 1 and 2.
All inputs are finite; a program needn't handle non-finite values.
Results may differ from a plain program's by a relative error of at most 0.00013.
Values sent between devices are 32-bit elements; how exact they have to be, the bound alone decides.
A program may use at most 64 MiB of HBM per device.

v0:
```python
import jax
import jax.numpy as jnp
from jax import lax
from jax.sharding import PartitionSpec as P

PANELS = 3


def spread(block, axis, owner):
    block = jnp.where(lax.axis_index(axis) == owner, block, jnp.zeros_like(block))
    return lax.psum(block, axis)


def inner_product(left, right):
    return lax.dot_general(
        left,
        right,
        (((0,), (0,)), ((), ())),
        precision=lax.Precision.HIGHEST,
        preferred_element_type=jnp.float32,
    )


def matmul(left, right):
    return jnp.dot(left, right, precision=lax.Precision.HIGHEST, preferred_element_type=jnp.float32)


def fetch_panel(slots, root):
    return spread(slots[0], "col", root)


def shards(eigvec, slots, roots, tfac):
    current = eigvec
    panels = [fetch_panel(slots, roots[index]) for index in range(PANELS)]
    for index in range(PANELS):
        summed = lax.psum(inner_product(panels[index], current), "row")
        scaled = matmul(tfac[index], summed)
        current = current - matmul(panels[index], scaled)
    return current


def solution(mesh):
    in_specs = (P("row", "col"), P("col", "row", None), P(), P())
    out_specs = P("row", "col")
    return jax.shard_map(shards, mesh=mesh, in_specs=in_specs, out_specs=out_specs, check_vma=False)
```

profile of v0, /device:TPU:1, one launch (start us, length us, event | category | flops | bytes accessed | tf_op | source)
XLA Modules:
  0.0 537.4 jit_solution(14417372556661301659)
XLA Ops:
  6.5 0.0 all-reduce.12.cloned.1.call-start
  6.5 1.4 fusion.9
  9.9 4.5 select_bitcast_fusion
  14.3 0.0 all-reduce.12.cloned.1.call-update
  14.4 0.0 all-reduce.6.cloned.1.call-start
  14.4 136.2 %all-reduce.12.cloned.1.call-done = (f32[2048,256]{1,0:T(8,128)}, f32[2048,256]{1,0:T(8,128)}, f32[2048,256]{1,0:T(8,128)}) async-done(((f32[2048,256]{1,0:T(8,128)}, f32[2048,256]{1,0:T(8,128)}, f32[2048,256]{1,0:T(8,128)}), (f32[2048,256]{1,0:T(8,128)}, f32[2048,256]{1,0:T(8,128)}, f32[2048,256]{1,0:T(8,128)})) %all-reduce.12.cloned.1.call-update) | async-done | bytes 6291472 | tf_op jit(solution)/shard_map/psum | solution.py:11
  150.7 0.0 copy-start.5
  150.7 0.0 copy-start.4
  150.7 7.4 %fusion.10 = f32[256,512]{1,0:T(8,128)} fusion(f32[2048,256]{1,0:T(8,128)} %get-tuple-element.5, f32[2048,512]{1,0:T(8,128)} %param.4), kind=kOutput, calls=%fused_computation.16 | convolution fusion | flops 3221225472 | bytes 6815744 | tf_op jit(solution)/shard_map/dot_general | solution.py:15
  158.1 0.0 all-reduce.6.cloned.1.call-update
  158.1 0.0 all-reduce.8.cloned.1.call-start
  158.1 110.8 %all-reduce.6.cloned.1.call-done = f32[256,512]{1,0:T(8,128)} async-done(((f32[256,512]{1,0:T(8,128)}), f32[256,512]{1,0:T(8,128)}) %all-reduce.6.cloned.1.call-update) | async-done | bytes 524304 | tf_op jit(solution)/shard_map/psum | solution.py:36
  269.0 0.0 copy-done.5
  269.0 2.0 fusion.4
  271.0 0.0 copy-done.4
  271.0 0.0 copy-start.3
  271.0 5.6 %convolution_subtract_fusion.2 = f32[2048,512]{1,0:T(8,128)S(1)} fusion(f32[2048,512]{1,0:T(8,128)} %param.4, f32[2048,256]{1,0:T(8,128)S(1)} %copy-done.4, f32[512,256]{1,0:T(8,128)S(1)} %fusion.4), kind=kOutput, calls=%fused_computation.2 | convolution fusion | flops 3222274048 | bytes 11010048 | tf_op jit(solution)/shard_map/dot_general | solution.py:25
  276.7 0.0 copy-start
  276.7 2.0 copy-done
  278.7 0.0 copy-done.3
  278.7 4.7 fusion.11
  283.4 0.0 all-reduce.8.cloned.1.call-update
  283.4 0.2 all-reduce.10.cloned.1.call-start
  283.6 110.9 %all-reduce.8.cloned.1.call-done = f32[256,512]{1,0:T(8,128)} async-done(((f32[256,512]{1,0:T(8,128)}), f32[256,512]{1,0:T(8,128)}) %all-reduce.8.cloned.1.call-update) | async-done | bytes 524304 | tf_op jit(solution)/shard_map/psum | solution.py:36
  394.5 2.0 fusion.2
  396.6 0.0 copy-start.2
  396.6 7.7 %convolution_subtract_fusion.1 = f32[2048,512]{1,0:T(8,128)S(1)} fusion(f32[2048,512]{1,0:T(8,128)} %copy-done, f32[2048,256]{1,0:T(8,128)} %get-tuple-element.6, f32[512,256]{1,0:T(8,128)S(1)} %fusion.2), kind=kOutput, calls=%fused_computation.1 | convolution fusion | flops 3222274048 | bytes 11010048 | tf_op jit(solution)/shard_map/dot_general | solution.py:25
  404.3 0.0 copy-start.1
  404.3 2.0 copy-done.1
  406.3 0.0 copy-done.2
  406.3 4.5 fusion.12
  410.8 0.0 all-reduce.10.cloned.1.call-update
  410.9 111.3 %all-reduce.10.cloned.1.call-done = f32[256,512]{1,0:T(8,128)} async-done(((f32[256,512]{1,0:T(8,128)}), f32[256,512]{1,0:T(8,128)}) %all-reduce.10.cloned.1.call-update) | async-done | bytes 524304 | tf_op jit(solution)/shard_map/psum | solution.py:36
  522.2 2.0 fusion
  524.2 6.6 %convolution_subtract_fusion = f32[2048,512]{1,0:T(8,128)} fusion(f32[2048,512]{1,0:T(8,128)} %copy-done.1, f32[2048,256]{1,0:T(8,128)S(1)} %copy-done.2, f32[512,256]{1,0:T(8,128)S(1)} %fusion), kind=kOutput, calls=%fused_computation | convolution fusion | flops 3222274048 | bytes 11010048 | tf_op jit(solution)/shard_map/dot_general | solution.py:25
Async XLA Ops:
  6.5 144.1 %all-reduce.12.cloned.1.call-start = ((), (), s32[]{:S(2)}) async-start(), calls=%async_computation.3 | async-start | bytes 12582912 | tf_op jit(solution)/shard_map/psum | solution.py:11
  14.4 254.6 %all-reduce.6.cloned.1.call-start = ((), (), s32[]{:S(2)}) async-start(), calls=%async_computation | async-start | bytes 1048576 | tf_op jit(solution)/shard_map/psum | solution.py:36
  150.7 118.3 %copy-start.5 = (f32[3,256,256]{2,1,0:T(8,128)S(1)}, f32[3,256,256]{2,1,0:T(8,128)}, u32[]{:S(2)}) copy-start(f32[3,256,256]{2,1,0:T(8,128)} %param.7) | copy-start | bytes 2359300
  150.7 120.4 %copy-start.4 = (f32[2048,256]{1,0:T(8,128)S(1)}, f32[2048,256]{1,0:T(8,128)}, u32[]{:S(2)}) copy-start(f32[2048,256]{1,0:T(8,128)} %get-tuple-element.5) | copy-start | bytes 6291460
  158.1 236.4 %all-reduce.8.cloned.1.call-start = ((), (), s32[]{:S(2)}) async-start(), calls=%async_computation.1 | async-start | bytes 1048576 | tf_op jit(solution)/shard_map/psum | solution.py:36
  271.0 7.7 %copy-start.3 = (f32[2048,256]{1,0:T(8,128)S(1)}, f32[2048,256]{1,0:T(8,128)}, u32[]{:S(2)}) copy-start(f32[2048,256]{1,0:T(8,128)} %get-tuple-element.6) | copy-start | bytes 6291460
  276.7 2.0 copy-start
  283.4 238.8 %all-reduce.10.cloned.1.call-start = ((), (), s32[]{:S(2)}) async-start(), calls=%async_computation.2 | async-start | bytes 1048576 | tf_op jit(solution)/shard_map/psum | solution.py:36
  396.6 9.8 %copy-start.2 = (f32[2048,256]{1,0:T(8,128)S(1)}, f32[2048,256]{1,0:T(8,128)}, u32[]{:S(2)}) copy-start(f32[2048,256]{1,0:T(8,128)} %get-tuple-element.7) | copy-start | bytes 6291460
  404.3 2.0 copy-start.1
Sparse Core Ops, SparseCore 0:
  14.5 136.1 all-reduce.11
  158.2 110.7 all-reduce.5
  283.5 110.9 all-reduce.7
  411.0 111.1 all-reduce.9
where the time goes:
time: 538 us; the launch traced here: 537 us
  waiting for transfers between devices  469 us (87%)
  matrix products  42.7 us (8%)
  between operations  15.1 us (3%)
  local copies, waits for them, and re-layouts  5.45 us (1%)
    psum x3, waiting for transfers between devices, shards(): summed = lax.psum(inner_product(panels[index], current), 'row')  333 us
    psum x1, waiting for transfers between devices, spread(): return lax.psum(block, axis)  136 us
    dot_general x6, matrix products, matmul(): jnp.dot(left, right, precision=lax.Precision.HIGHEST, preferred_element_t...  26.1 us
    dot_general x3, matrix products, inner_product(): lax.dot_general(left, right, (((0,), (0,)), ((), ())), precision=lax.Prec...  16.6 us
  transfers between devices with their start and end apart: 4, of which 4 were waited for; matrix products, arithmetic and copies ran while one was open for 0% of the time, Pallas kernels for 0%

commit v1 on v0

v1 whole, which is shorter than its diff:
```python
import functools

import jax
import jax.numpy as jnp
from jax import lax
from jax.experimental import pallas as pl
from jax.experimental.pallas import tpu as pltpu
from jax.sharding import PartitionSpec as P

PANELS = 3
NB = 256
SIDE = 4
TREES = 4
HOPS = 5
CHUNK = 32
SKEW = 4
MESH = pl.DeviceIdType.MESH

FEED = {
    (0, 1): 0, (0, 2): 0, (0, 3): 0, (1, 0): 2, (1, 1): 2, (1, 2): 2, (1, 3): 2, (2, 0): 2,
    (2, 1): 1, (2, 2): 1, (2, 3): 2, (3, 0): 2, (3, 1): 1, (3, 2): 3, (3, 3): 3,
}
STEP = ((1, 0), (0, 1), (-1, 0), (0, -1))


def turn(node, times):
    for _ in range(times):
        node = (-node[1] % SIDE, node[0])
    return node


def build_tables():
    depth = {(0, 0): 0}

    def find(node):
        if node not in depth:
            dx, dy = STEP[FEED[node]]
            depth[node] = 1 + find(((node[0] - dx) % SIDE, (node[1] - dy) % SIDE))
        return depth[node]

    child = [[0] * 4 for _ in range(TREES)]
    deeper = [[0] * HOPS for _ in range(TREES)]
    for node in FEED:
        find(node)
        dx, dy = STEP[FEED[node]]
        parent = ((node[0] - dx) % SIDE, (node[1] - dy) % SIDE)
        for t in range(TREES):
            px, py = turn(parent, t)
            child[t][(FEED[node] + t) % 4] |= 1 << (px * SIDE + py)
            nx, ny = turn(node, t)
            for level in range(depth[node]):
                deeper[t][level] |= 1 << (nx * SIDE + ny)
    return child, deeper


CHILD, DEEPER = build_tables()


def bit(mask, place):
    return lax.rem(lax.shift_right_logical(jnp.int32(mask), place), 2)


def spread_kernel(roots, slot_ref, panel_ref, send_sem, recv_sem, load_sem):
    col = lax.axis_index("col")
    x, y = col // SIDE, lax.rem(col, SIDE)
    near = [
        lax.rem(x + 1, SIDE) * SIDE + y,
        x * SIDE + lax.rem(y + 1, SIDE),
        lax.rem(x + 3, SIDE) * SIDE + y,
        x * SIDE + lax.rem(y + 3, SIDE),
    ]
    rows = panel_ref.shape[1]
    count = rows // (TREES * CHUNK)

    barrier = pltpu.get_barrier_semaphore()
    for d in range(4):
        pl.semaphore_signal(barrier, inc=1, device_id={"col": near[d]}, device_id_type=MESH)

    place = []
    for p in range(PANELS):
        rx, ry = roots[p] // SIDE, roots[p] % SIDE
        place.append(lax.rem(x - rx + SIDE, SIDE) * SIDE + lax.rem(y - ry + SIDE, SIDE))
        load = pltpu.make_async_copy(slot_ref.at[0], panel_ref.at[p], load_sem)

        @pl.when(place[p] == 0)
        def _():
            load.start()
            load.wait()

    pl.semaphore_wait(barrier, 4)
    level = [[sum(bit(m, place[p]) for m in DEEPER[t]) for t in range(TREES)] for p in range(PANELS)]

    def piece(p, c, t, d):
        block = panel_ref.at[p, pl.ds(pl.multiple_of((c * TREES + t) * CHUNK, CHUNK), CHUNK)]
        return pltpu.make_async_remote_copy(
            src_ref=block,
            dst_ref=block,
            send_sem=send_sem.at[p, t, d],
            recv_sem=recv_sem.at[p, c, t],
            device_id={"col": near[d]},
            device_id_type=MESH,
        )

    def step(s, carry):
        for p in range(PANELS):
            for t in range(TREES):
                c = s - p * count - SKEW * level[p][t]

                @pl.when(jnp.logical_and(c >= 0, c < count))
                def _():
                    @pl.when(place[p] != 0)
                    def _():
                        piece(p, c, t, 0).wait_recv()

                    for d in range(4):
                        @pl.when(bit(CHILD[t][d], place[p]) == 1)
                        def _():
                            piece(p, c, t, d).start()
        return carry

    lax.fori_loop(0, PANELS * count + SKEW * HOPS, step, 0)

    for p in range(PANELS):
        for t in range(TREES):
            for d in range(4):
                @pl.when(bit(CHILD[t][d], place[p]) == 1)
                def _():
                    whole = panel_ref.at[p, pl.ds(0, rows // TREES)]
                    pltpu.make_async_remote_copy(
                        src_ref=whole,
                        dst_ref=whole,
                        send_sem=send_sem.at[p, t, d],
                        recv_sem=recv_sem.at[p, 0, t],
                        device_id={"col": near[d]},
                        device_id_type=MESH,
                    ).wait_send()


def spread(roots, key, slot):
    rows = slot.shape[1]
    count = rows // (TREES * CHUNK)
    return pl.pallas_call(
        functools.partial(spread_kernel, roots),
        out_shape=jax.ShapeDtypeStruct((PANELS, rows, NB), jnp.float32),
        in_specs=[pl.BlockSpec(memory_space=pl.ANY)],
        out_specs=pl.BlockSpec(memory_space=pltpu.VMEM),
        scratch_shapes=[
            pltpu.SemaphoreType.DMA((PANELS, TREES, 4)),
            pltpu.SemaphoreType.DMA((PANELS, count, TREES)),
            pltpu.SemaphoreType.DMA,
        ],
        compiler_params=pltpu.CompilerParams(collective_id=key, has_side_effects=True),
        name="spread_%d" % key,
    )(slot)


def product(left, right, dims):
    return lax.dot_general(
        left, right, (dims, ((), ())), precision=lax.Precision.HIGH, preferred_element_type=jnp.float32
    )


def shards(eigvec, slots, roots, tfac):
    panels = lax.cond(
        roots[0] == 14,
        functools.partial(spread, (14, 15, 0), 0),
        functools.partial(spread, (15, 0, 1), 1),
        slots,
    )
    first, second, third = panels[0], panels[1], panels[2]
    down = ((0,), (0,))
    inner = [product(v, eigvec, down) for v in (first, second, third)]
    cross = [product(second, first, down), product(third, first, down), product(third, second, down)]
    inner, cross = lax.psum((inner, cross), "row")
    flat = ((1,), (0,))
    y1 = product(tfac[0], inner[0], flat)
    y2 = product(tfac[1], inner[1] - product(cross[0], y1, flat), flat)
    y3 = product(tfac[2], inner[2] - product(cross[1], y1, flat) - product(cross[2], y2, flat), flat)
    return eigvec - (product(first, y1, flat) + product(second, y2, flat) + product(third, y3, flat))


def solution(mesh):
    in_specs = (P("row", "col"), P("col", "row", None), P(), P())
    out_specs = P("row", "col")
    return jax.shard_map(shards, mesh=mesh, in_specs=in_specs, out_specs=out_specs, check_vma=False)
```

time: 538 us -> 241 us (0.45)
  waiting for transfers between devices: 469 us -> 131 us
  Pallas kernels: 0 us -> 58.9 us
  matrix products: 42.7 us -> 35.9 us
    psum x4 -> x1, waiting for transfers between devices: 469 us -> 131 us  [shards(): inner, cross = lax.psum((inner, cross), 'row')]
    pallas_call x0 -> x1, Pallas kernels: none -> 58.9 us  [spread(): pl.pallas_call(functools.partial(spread_kernel, roots), out_shape=jax.Sha...]
    dot_general x9 -> x15, matrix products: 42.7 us -> 35.9 us  [product(): lax.dot_general(left, right, (dims, ((), ())), precision=lax.Precision.HI...]
  transfers between devices with their start and end apart: 4 -> 1, of which waited for: 4 -> 1; matrix products, arithmetic and copies ran while one was open for 0% -> 0% of each run, Pallas kernels for 0% -> 0%
where the time goes in v1:
time: 241 us
  waiting for transfers between devices  131 us (54%)
  Pallas kernels  58.9 us (24%)
  matrix products  35.9 us (15%)
  between operations  14.2 us (6%)
    psum x1, waiting for transfers between devices, shards(): inner, cross = lax.psum((inner, cross), 'row')  131 us
    pallas_call x1, Pallas kernels, spread(): pl.pallas_call(functools.partial(spread_kernel, roots), out_shape=jax.Sha...  58.9 us
    dot_general x15, matrix products, product(): lax.dot_general(left, right, (dims, ((), ())), precision=lax.Precision.HI...  35.9 us
  transfers between devices with their start and end apart: 1, of which 1 were waited for; matrix products, arithmetic and copies ran while one was open for 0% of the time, Pallas kernels for 0%

profile of v1, /device:TPU:1, one launch (start us, length us, event | category | flops | bytes accessed | tf_op | source)
XLA Modules:
  0.0 241.0 jit_solution(11966040101991980317)
XLA Ops:
  6.5 0.0 all-reduce.3.cloned.1.call-start
  7.2 59.1 %conditional.1 = (f32[3,2048,256]{2,1,0:T(8,128)}) conditional(s32[]{:T(128)} %bitcast, f32[1,2048,256]{2,1,0:T(8,128)} %param.7, f32[1,2048,256]{2,1,0:T(8,128)} %param.7), branch_computations={%region_0.0_spmd, %region_1.0_spmd} | conditional | bytes 8 | solution.py:164
  7.2 58.9 %spread_1.3 = f32[3,2048,256]{2,1,0:T(8,128)} custom-call(f32[1,2048,256]{2,1,0:T(8,128)} %slot_ref), custom_call_target="tpu_custom_call" | custom-call | tf_op jit(solution)/shard_map/cond/branch_0_fun/spread_1/pallas_call | solution.py:142
  66.3 0.0 copy-start
  66.3 4.9 %fusion.10 = f32[256,256]{1,0:T(8,128)} fusion(f32[3,2048,256]{2,1,0:T(8,128)} %get-tuple-element.48), kind=kOutput, calls=%fused_computation.11 | convolution fusion | flops 805306368 | bytes 4456448 | tf_op jit(solution)/shard_map/dot_general | solution.py:158
  71.2 0.0 copy-start.1
  71.2 4.9 %fusion.1 = f32[256,256]{1,0:T(8,128)} fusion(f32[3,2048,256]{2,1,0:T(8,128)} %get-tuple-element.48), kind=kOutput, calls=%fused_computation.2 | convolution fusion | flops 805306368 | bytes 4456448 | tf_op jit(solution)/shard_map/dot_general | solution.py:158
  76.1 0.0 copy-done
  76.1 2.6 %fusion.3 = f32[256,256]{1,0:T(8,128)} fusion(f32[3,2048,256]{2,1,0:T(8,128)S(1)} %copy-done), kind=kOutput, calls=%fused_computation.4 | convolution fusion | flops 805306368 | bytes 4456448 | tf_op jit(solution)/shard_map/dot_general | solution.py:158
  78.7 0.0 copy-done.1
  78.7 2.9 %fusion.5 = f32[256,512]{1,0:T(8,128)} fusion(f32[2048,512]{1,0:T(8,128)S(1)} %copy-done.1, f32[3,2048,256]{2,1,0:T(8,128)S(1)} %copy-done), kind=kOutput, calls=%fused_computation.6 | convolution fusion | flops 1610612736 | bytes 6815744 | tf_op jit(solution)/shard_map/dot_general | solution.py:158
  81.6 2.9 %fusion.12 = f32[256,512]{1,0:T(8,128)} fusion(f32[2048,512]{1,0:T(8,128)S(1)} %copy-done.1, f32[3,2048,256]{2,1,0:T(8,128)S(1)} %copy-done), kind=kOutput, calls=%fused_computation.13 | convolution fusion | flops 1610612736 | bytes 6815744 | tf_op jit(solution)/shard_map/dot_general | solution.py:158
  84.5 0.0 copy-start.3
  84.5 2.8 %fusion.18 = f32[256,512]{1,0:T(8,128)} fusion(f32[2048,512]{1,0:T(8,128)S(1)} %copy-done.1, f32[3,2048,256]{2,1,0:T(8,128)S(1)} %copy-done), kind=kOutput, calls=%fused_computation.19 | convolution fusion | flops 1610612736 | bytes 6815744 | tf_op jit(solution)/shard_map/dot_general | solution.py:158
  87.4 0.0 slice-start
  87.4 0.0 all-reduce.3.cloned.1.call-update
  87.4 131.0 %all-reduce.3.cloned.1.call-done = (f32[256,512]{1,0:T(8,128)}, f32[256,512]{1,0:T(8,128)}, f32[256,256]{1,0:T(8,128)}, f32[256,512]{1,0:T(8,128)}, f32[256,256]{1,0:T(8,128)}, /*index=5*/f32[256,256]{1,0:T(8,128)}) async-done(((f32[256,512]{1,0:T(8,128)}, f32[256,512]{1,0:T(8,128)}, f32[256,256]{1,0:T(8,128)}, f32[256,512]{1,0:T(8,128)}, f32[256,256]{1,0:T(8,128)}, /*index=5*/f32[256,256]{1,0:T(8,128)}), ...) | async-done | bytes 2359312 | tf_op jit(solution)/shard_map/psum | solution.py:174
  218.4 0.0 copy-start.5
  218.4 0.0 copy-start.8
  218.4 0.0 copy-done.3
  218.4 1.7 fusion.36
  220.1 0.0 slice-start.1
  220.2 3.9 %fusion.16 = f32[2048,512]{1,0:T(8,128)S(1)} fusion(f32[512,256]{1,0:T(8,128)S(1)} %fusion.36, f32[3,2048,256]{2,1,0:T(8,128)} %get-tuple-element.48), kind=kOutput, calls=%fused_computation.17 | convolution fusion | flops 1610612736 | bytes 6815744 | tf_op jit(solution)/shard_map/dot_general | solution.py:158
  224.1 0.0 copy-done.5
  224.1 0.0 copy-done.8
  224.1 0.4 convolution_subtract_fusion.2
  224.5 0.0 copy-start.4
  224.5 0.0 copy-start.7
  224.6 0.6 fusion.34
  225.2 0.0 slice-done
  225.2 0.0 slice-done.1
  225.2 0.0 copy-start.6
  225.2 1.9 fusion.8
  227.2 0.0 copy-start.2
  227.2 0.0 copy-done.4
  227.2 0.0 copy-done.7
  227.2 0.4 convolution_subtract_fusion.1
  227.6 0.0 copy-done.6
  227.6 0.4 convolution_subtract_fusion
  228.1 0.6 fusion.32
  228.7 0.6 copy-done.2
  229.3 4.8 %add_subtract_fusion = f32[2048,512]{1,0:T(8,128)} fusion(f32[2048,512]{1,0:T(8,128)S(1)} %copy-done.2, f32[2048,512]{1,0:T(8,128)S(1)} %fusion.16, f32[2048,512]{1,0:T(8,128)S(1)} %fusion.8, f32[512,256]{1,0:T(8,128)S(1)} %fusion.32, f32[3,2048,256]{2,1,0:T(8,128)S(1)} %bitcast.54), kind=kOutput, calls=%fused_computation | convolution fusion | flops 1613758464 | bytes 19398656 | tf_op jit(solution)/shard_map/dot_general | solution.py:158
  (1 shorter events, 0.0 us)
Async XLA Ops:
  6.5 211.9 %all-reduce.3.cloned.1.call-start = ((), (), s32[]{:S(2)}) async-start(), calls=%async_computation | async-start | bytes 4718592 | tf_op jit(solution)/shard_map/psum | solution.py:174
  66.3 9.8 %copy-start = (f32[3,2048,256]{2,1,0:T(8,128)S(1)}, f32[3,2048,256]{2,1,0:T(8,128)}, u32[]{:S(2)}) copy-start(f32[3,2048,256]{2,1,0:T(8,128)} %get-tuple-element.48) | copy-start | bytes 18874372
  71.2 7.5 %copy-start.1 = (f32[2048,512]{1,0:T(8,128)S(1)}, f32[2048,512]{1,0:T(8,128)}, u32[]{:S(2)}) copy-start(f32[2048,512]{1,0:T(8,128)} %param.6) | copy-start | bytes 12582916
  84.5 133.9 %copy-start.3 = (f32[3,256,256]{2,1,0:T(8,128)S(1)}, f32[3,256,256]{2,1,0:T(8,128)}, u32[]{:S(2)}) copy-start(f32[3,256,256]{2,1,0:T(8,128)} %param.9) | copy-start | bytes 2359300
  87.4 137.8 %slice-start = ((s8[6291456]{0:T(1024)(128)(4,1)}), s8[2097152]{0:T(1024)(128)(4,1)S(1)}, s32[]{:S(2)}) async-start(s8[6291456]{0:T(1024)(128)(4,1)} %bitcast.53), calls=%async_computation.1 | async-start | bytes 4194304
  218.4 5.7 %copy-start.5 = (f32[256,512]{1,0:T(8,128)S(1)}, f32[256,512]{1,0:T(8,128)}, u32[]{:S(2)}) copy-start(f32[256,512]{1,0:T(8,128)} %get-tuple-element.37) | copy-start | bytes 1572868
  218.4 5.7 %copy-start.8 = (f32[256,256]{1,0:T(8,128)S(1)}, f32[256,256]{1,0:T(8,128)}, u32[]{:S(2)}) copy-start(f32[256,256]{1,0:T(8,128)} %get-tuple-element.38) | copy-start | bytes 786436
  220.1 5.1 %slice-start.1 = ((s8[6291456]{0:T(1024)(128)(4,1)}), s8[4194304]{0:T(1024)(128)(4,1)S(1)}, s32[]{:S(2)}) async-start(s8[6291456]{0:T(1024)(128)(4,1)} %bitcast.53), calls=%async_computation.2 | async-start | bytes 8388608
  224.5 2.6 %copy-start.4 = (f32[256,512]{1,0:T(8,128)S(1)}, f32[256,512]{1,0:T(8,128)}, u32[]{:S(2)}) copy-start(f32[256,512]{1,0:T(8,128)} %get-tuple-element.39) | copy-start | bytes 1572868
  224.5 2.6 %copy-start.7 = (f32[256,256]{1,0:T(8,128)S(1)}, f32[256,256]{1,0:T(8,128)}, u32[]{:S(2)}) copy-start(f32[256,256]{1,0:T(8,128)} %get-tuple-element.40) | copy-start | bytes 786436
  225.2 2.4 %copy-start.6 = (f32[256,256]{1,0:T(8,128)S(1)}, f32[256,256]{1,0:T(8,128)}, u32[]{:S(2)}) copy-start(f32[256,256]{1,0:T(8,128)} %get-tuple-element.41) | copy-start | bytes 786436
  227.2 2.2 copy-start.2
Sparse Core Ops, SparseCore 0:
  87.5 130.8 all-reduce.2

commit v2 on v1

v2 whole, which is shorter than its diff:
```python
import functools

import jax
import jax.numpy as jnp
from jax import lax
from jax.experimental import pallas as pl
from jax.experimental.pallas import tpu as pltpu
from jax.sharding import PartitionSpec as P

PANELS = 3
NB = 256
SIDE = 4
TREES = 4
HOPS = 5
CHUNK = 32
SKEW = 4
GRID = SIDE * SIDE
DEPTH = 8
HALF = NB // 2
PREP = 16
GAPS = (3, 14, 26, 29)
MESH = pl.DeviceIdType.MESH

FEED = {
    (0, 1): 0, (0, 2): 0, (0, 3): 0, (1, 0): 2, (1, 1): 2, (1, 2): 2, (1, 3): 2, (2, 0): 2,
    (2, 1): 1, (2, 2): 1, (2, 3): 2, (3, 0): 2, (3, 1): 1, (3, 2): 3, (3, 3): 3,
}
STEP = ((1, 0), (0, 1), (-1, 0), (0, -1))


def turn(node, times):
    for _ in range(times):
        node = (-node[1] % SIDE, node[0])
    return node


def build_tables():
    depth = {(0, 0): 0}

    def find(node):
        if node not in depth:
            dx, dy = STEP[FEED[node]]
            depth[node] = 1 + find(((node[0] - dx) % SIDE, (node[1] - dy) % SIDE))
        return depth[node]

    child = [[0] * 4 for _ in range(TREES)]
    deeper = [[0] * HOPS for _ in range(TREES)]
    for node in FEED:
        find(node)
        dx, dy = STEP[FEED[node]]
        parent = ((node[0] - dx) % SIDE, (node[1] - dy) % SIDE)
        for t in range(TREES):
            px, py = turn(parent, t)
            child[t][(FEED[node] + t) % 4] |= 1 << (px * SIDE + py)
            nx, ny = turn(node, t)
            for level in range(depth[node]):
                deeper[t][level] |= 1 << (nx * SIDE + ny)
    return child, deeper


CHILD, DEEPER = build_tables()


def bit(mask, place):
    return lax.rem(lax.shift_right_logical(jnp.int32(mask), place), 2)


def split(value):
    high = value.astype(jnp.bfloat16)
    return high, (value - high.astype(jnp.float32)).astype(jnp.bfloat16)


def dot(left, right, turned=False):
    dims = ((1,), (1,)) if turned else ((1,), (0,))
    return lax.dot_general(left, right, (dims, ((), ())), preferred_element_type=jnp.float32)


def dot3(left, right, turned=False):
    return dot(left[0], right[0], turned) + (dot(left[0], right[1], turned) + dot(left[1], right[0], turned))


def kernel(
    roots, slot_ref, x_ref, t_ref, out_ref,
    panel, state, xh, xl, vh, vl, acc, fromcore, chip, fromz, crossz, total, cross, yth, ytl, yh, yl,
    tree_send, tree_recv, load_sem, core_send, core_recv, z_send, z_recv, cz_send, cz_recv,
    all_send, all_recv, relay_send, relay_recv, plane_send, plane_recv, pass_send, pass_recv, out_sem,
):
    row, col = lax.axis_index("row"), lax.axis_index("col")
    x, y = col // SIDE, lax.rem(col, SIDE)
    z, core = row // 2, lax.rem(row, 2)
    near = [
        lax.rem(x + 1, SIDE) * SIDE + y,
        x * SIDE + lax.rem(y + 1, SIDE),
        lax.rem(x + 3, SIDE) * SIDE + y,
        x * SIDE + lax.rem(y + 3, SIDE),
    ]
    mate = {"row": z * 2 + 1 - core}
    rows, width = state.shape
    block = TREES * CHUNK
    count = rows // block

    def zplus(k):
        return lax.rem(z + k, DEPTH)

    load_x = pltpu.make_async_copy(x_ref, state, load_sem.at[0])
    load_x.start()

    barrier = pltpu.get_barrier_semaphore()
    for k in range(1, GRID):
        pl.semaphore_signal(barrier, inc=1, device_id={"col": lax.rem(col + k, GRID)}, device_id_type=MESH)
    for k in range(1, DEPTH):
        pl.semaphore_signal(barrier, inc=1, device_id={"row": zplus(k) * 2 + core}, device_id_type=MESH)
    pl.semaphore_signal(barrier, inc=1, device_id=mate, device_id_type=MESH)

    place = []
    for p in range(PANELS):
        rx, ry = roots[p] // SIDE, roots[p] % SIDE
        place.append(lax.rem(x - rx + SIDE, SIDE) * SIDE + lax.rem(y - ry + SIDE, SIDE))
        load = pltpu.make_async_copy(slot_ref.at[0], panel.at[p], load_sem.at[1])

        @pl.when(place[p] == 0)
        def _():
            load.start()
            load.wait()

    pl.semaphore_wait(barrier, GRID - 1 + DEPTH - 1 + 1)
    level = [[sum(bit(m, place[p]) for m in DEEPER[t]) for t in range(TREES)] for p in range(PANELS)]

    def piece(p, c, t, d):
        ref = panel.at[p, pl.ds(pl.multiple_of((c * TREES + t) * CHUNK, CHUNK), CHUNK)]
        return pltpu.make_async_remote_copy(
            src_ref=ref, dst_ref=ref, send_sem=tree_send.at[p, t, d], recv_sem=tree_recv.at[p, c, t],
            device_id={"col": near[d]}, device_id_type=MESH,
        )

    def spread(s):
        for p in range(PANELS):
            for t in range(TREES):
                c = s - p * count - SKEW * level[p][t]

                @pl.when(jnp.logical_and(c >= 0, c < count))
                def _():
                    @pl.when(place[p] != 0)
                    def _():
                        piece(p, c, t, 0).wait_recv()

                    for d in range(4):
                        @pl.when(bit(CHILD[t][d], place[p]) == 1)
                        def _():
                            piece(p, c, t, d).start()

    part = rows // PREP

    def prepare(i):
        at = pl.ds(pl.multiple_of(i * part, part), part)
        high, low = split(state[at, :].T)
        xh[0:width, at] = high
        xl[0:width, at] = low

    pick = lax.broadcasted_iota(jnp.int32, (16, NB), 0)
    pick = jnp.where(pick < 8, 0, HALF - 8) + pick + 8 * col
    pick = jnp.where(pick == lax.broadcasted_iota(jnp.int32, (16, NB), 1), 1.0, 0.0).astype(jnp.bfloat16)

    def gather(p, c):
        at = pl.ds(pl.multiple_of(c * block, block), block)
        high, low = split(panel[p, at, :])
        vh[p, at, :] = high
        vl[p, at, :] = low
        tall = width if p == 0 else width + 32
        acc[p, 0:tall, :] += dot3((xh[0:tall, at], xl[0:tall, at]), (high, low))
        if p < PANELS - 1:
            strip = slice(width + 16 * p, width + 16 * p + 16)
            xh[strip, at] = dot(pick, high, True).astype(jnp.bfloat16)
            xl[strip, at] = dot(pick, low, True).astype(jnp.bfloat16)

    def remote(src, dst, send, recv, device):
        return pltpu.make_async_remote_copy(
            src_ref=src, dst_ref=dst, send_sem=send, recv_sem=recv, device_id=device, device_id_type=MESH
        )

    def to_mate(p):
        copies = [remote(acc.at[p, pl.ds(pl.multiple_of((1 - core) * half, half), half)], fromcore.at[p, pl.ds(0, half)],
                         core_send.at[p, 0], core_recv.at[p, 0], mate)]
        if p:
            copies.append(remote(acc.at[p, pl.ds(width, 32)], fromcore.at[p, pl.ds(half, 32)],
                                 core_send.at[p, 1], core_recv.at[p, 1], mate))
        return copies

    half = width // 2
    slice_rows = half // DEPTH

    def z_out(p):
        copies = []
        for k in range(1, DEPTH):
            there = {"row": zplus(k) * 2 + core}
            copies.append(remote(chip.at[p, pl.ds(pl.multiple_of(zplus(k) * slice_rows, slice_rows), slice_rows)],
                                 fromz.at[p, k], z_send.at[p, k], z_recv.at[p, k], there))
            if p:
                copies.append(remote(chip.at[p, pl.ds(half, 16)], crossz.at[p - 1, k],
                                     cz_send.at[p, k], cz_recv.at[p, k], there))
        return copies

    def mine(p, k):
        at = core * half + zplus(DEPTH - k) * slice_rows
        return total.at[p, pl.ds(pl.multiple_of(at, slice_rows), slice_rows)]

    def all_out(p):
        return [remote(mine(p, 0), mine(p, 0), all_send.at[p, k], all_recv.at[p, k], {"row": zplus(k) * 2 + core})
                for k in range(1, DEPTH)]

    def relay_out(p, k):
        return remote(mine(p, k), mine(p, k), relay_send.at[p, k], relay_recv.at[p, k], mate)

    def plane_out(p):
        ref = cross.at[p - 1, core, col]
        return [remote(ref, ref, plane_send.at[p, k], plane_recv.at[p, k], {"col": lax.rem(col + k, GRID)})
                for k in range(1, GRID)]

    def pass_out(p):
        ref = cross.at[p - 1, core]
        return remote(ref, ref, pass_send.at[p], pass_recv.at[p], mate)

    def stage_a(p):
        for copy in to_mate(p):
            copy.start()

    def stage_b(p):
        for copy in to_mate(p):
            copy.wait_recv()
        chip[p, 0:half, :] = acc[p, pl.ds(pl.multiple_of(core * half, half), half), :] + fromcore[p, 0:half, :]
        if p:
            for q in range(2):
                at = pl.multiple_of(16 * q + 8 * core, 8)
                chip[p, half + 8 * q : half + 8 * q + 8, :] = (
                    acc[p, pl.ds(width + at, 8), :] + fromcore[p, pl.ds(half + at, 8), :]
                )
        for copy in z_out(p):
            copy.start()

    def stage_d(p):
        for copy in z_out(p):
            copy.wait_recv()
        own = chip[p, pl.ds(pl.multiple_of(z * slice_rows, slice_rows), slice_rows), :]
        for k in range(1, DEPTH):
            own = own + fromz[p, k]
        at = pl.multiple_of(core * half + z * slice_rows, slice_rows)
        total[p, pl.ds(at, slice_rows), :] = own
        for copy in all_out(p):
            copy.start()
        relay_out(p, 0).start()
        if p:
            for q in range(2):
                own = chip[p, half + 8 * q : half + 8 * q + 8, :]
                for k in range(1, DEPTH):
                    own = own + crossz[p - 1, k, 8 * q : 8 * q + 8, :]
                cross[p - 1, core, col, q] = own
            for copy in plane_out(p):
                copy.start()

    def stage_f(p):
        for k, copy in enumerate(all_out(p), 1):
            copy.wait_recv()
            relay_out(p, k).start()
        if p:
            for copy in plane_out(p):
                copy.wait_recv()
            pass_out(p).start()

    def stage_g(p):
        for k in range(DEPTH):
            relay_out(p, k).wait_recv()
        if p:
            pass_out(p).wait_recv()
        inner = total[p]
        for q in range(p):
            mixed = cross[p - 1, :, :, q].reshape(NB, NB)
            inner = inner - dot3((yth[q], ytl[q]), split(mixed))
        scaled = dot3(split(inner), split(t_ref[p]), True)
        if p < PANELS - 1:
            yth[p], ytl[p] = split(scaled)
        yh[...], yl[...] = split(scaled.T)

        def update(i, carry):
            at = pl.ds(pl.multiple_of(i * 256, 256), 256)
            state[at, :] = state[at, :] - dot3((vh[p, at, :], vl[p, at, :]), (yh[...], yl[...]))
            if p == PANELS - 1:
                pltpu.make_async_copy(state.at[at], out_ref.at[at], out_sem.at[i]).start()
            return carry

        lax.fori_loop(0, rows // 256, update, 0)

    zeros = jnp.zeros((32, rows), jnp.bfloat16)
    xh[width : width + 32, :] = zeros
    xl[width : width + 32, :] = zeros
    acc[...] = jnp.zeros_like(acc)
    load_x.wait()

    fill = SKEW * HOPS
    steps = PANELS * count + fill
    plan = []
    for p in range(PANELS):
        end = (p + 1) * count + fill
        for stage, gap in ((stage_a, 0), (stage_b, GAPS[0]), (stage_d, GAPS[1]), (stage_f, GAPS[2]), (stage_g, GAPS[3])):
            plan.append((end + gap, p, stage))
    plan.sort(key=lambda entry: entry[:2])
    late = [entry for entry in plan if entry[0] >= steps]
    plan = [entry for entry in plan if entry[0] < steps]
    cuts = sorted({0, min(PREP, fill), fill, steps} | {fill + p * count for p in range(1, PANELS)} | {entry[0] for entry in plan})
    for low, high in zip(cuts, cuts[1:]):
        for step, p, stage in plan:
            if step == low:
                stage(p)

        def turn_step(s, carry):
            spread(s)
            if low < PREP and low < fill:
                prepare(s)
            if low >= fill:
                p = (low - fill) // count
                gather(p, s - fill - p * count)
            return carry

        lax.fori_loop(low, high, turn_step, 0)

    order = [(stage_a, 2), (stage_b, 1), (stage_d, 0), (stage_d, 1), (stage_b, 2), (stage_f, 0), (stage_g, 0), (stage_f, 1),
             (stage_g, 1), (stage_d, 2), (stage_f, 2), (stage_g, 2)]
    pending = {(stage, p) for _, p, stage in late}
    for stage, p in order:
        if (stage, p) in pending:
            stage(p)

    for p in range(PANELS):
        for t in range(TREES):
            for d in range(4):
                @pl.when(bit(CHILD[t][d], place[p]) == 1)
                def _():
                    whole = panel.at[p, pl.ds(0, rows // TREES)]
                    remote(whole, whole, tree_send.at[p, t, d], tree_recv.at[p, 0, t], {"col": near[d]}).wait_send()
        for copy in to_mate(p) + z_out(p) + all_out(p) + [relay_out(p, k) for k in range(DEPTH)]:
            copy.wait_send()
        if p:
            for copy in plane_out(p) + [pass_out(p)]:
                copy.wait_send()
    for i in range(rows // 256):
        at = pl.ds(i * 256, 256)
        pltpu.make_async_copy(state.at[at], out_ref.at[at], out_sem.at[i]).wait()


def transform(roots, key, slot, eigvec, tfac):
    rows, width = eigvec.shape
    count = rows // (TREES * CHUNK)
    f32, bf16 = jnp.float32, jnp.bfloat16
    dma = pltpu.SemaphoreType.DMA
    return pl.pallas_call(
        functools.partial(kernel, roots),
        out_shape=jax.ShapeDtypeStruct((rows, width), f32),
        in_specs=[pl.BlockSpec(memory_space=pl.ANY), pl.BlockSpec(memory_space=pl.ANY), pl.BlockSpec(memory_space=pltpu.VMEM)],
        out_specs=pl.BlockSpec(memory_space=pl.ANY),
        scratch_shapes=[
            pltpu.VMEM((PANELS, rows, NB), f32),
            pltpu.VMEM((rows, width), f32),
            pltpu.VMEM((width + 32, rows), bf16),
            pltpu.VMEM((width + 32, rows), bf16),
            pltpu.VMEM((PANELS, rows, NB), bf16),
            pltpu.VMEM((PANELS, rows, NB), bf16),
            pltpu.VMEM((PANELS, width + 32, NB), f32),
            pltpu.VMEM((PANELS, width // 2 + 32, NB), f32),
            pltpu.VMEM((PANELS, width // 2 + 16, NB), f32),
            pltpu.VMEM((PANELS, DEPTH, width // 2 // DEPTH, NB), f32),
            pltpu.VMEM((PANELS - 1, DEPTH, 16, NB), f32),
            pltpu.VMEM((PANELS, width, NB), f32),
            pltpu.VMEM((PANELS - 1, 2, GRID, 2, 8, NB), f32),
            pltpu.VMEM((PANELS - 1, width, NB), bf16),
            pltpu.VMEM((PANELS - 1, width, NB), bf16),
            pltpu.VMEM((NB, width), bf16),
            pltpu.VMEM((NB, width), bf16),
            dma((PANELS, TREES, 4)),
            dma((PANELS, count, TREES)),
            dma((2,)),
            dma((PANELS, 2)), dma((PANELS, 2)),
            dma((PANELS, DEPTH)), dma((PANELS, DEPTH)),
            dma((PANELS, DEPTH)), dma((PANELS, DEPTH)),
            dma((PANELS, DEPTH)), dma((PANELS, DEPTH)),
            dma((PANELS, DEPTH)), dma((PANELS, DEPTH)),
            dma((PANELS, GRID)), dma((PANELS, GRID)),
            dma((PANELS,)), dma((PANELS,)),
            dma((rows // 256,)),
        ],
        compiler_params=pltpu.CompilerParams(
            collective_id=key, has_side_effects=True, vmem_limit_bytes=60 << 20
        ),
        name="transform_%d" % key,
    )(slot, eigvec, tfac)


def shards(eigvec, slots, roots, tfac):
    return lax.cond(
        roots[0] == GRID - 2,
        functools.partial(transform, (GRID - 2, GRID - 1, 0), 0),
        functools.partial(transform, (GRID - 1, 0, 1), 1),
        slots, eigvec, tfac,
    )


def solution(mesh):
    in_specs = (P("row", "col"), P("col", "row", None), P(), P())
    out_specs = P("row", "col")
    return jax.shard_map(shards, mesh=mesh, in_specs=in_specs, out_specs=out_specs, check_vma=False)
```

time: 241 us -> 117 us (0.49)
  waiting for transfers between devices: 131 us -> 0 us
  Pallas kernels: 58.9 us -> 111 us
  matrix products: 35.9 us -> 0 us
  between operations: 14.2 us -> 0.66 us
  local copies, waits for them, and re-layouts: 0.68 us -> 4.64 us
    psum x1 -> x0, waiting for transfers between devices: 131 us -> none  [shards(): inner, cross = lax.psum((inner, cross), 'row')]
    pallas_call x1, Pallas kernels: 58.9 us -> 111 us  [transform(): pl.pallas_call(functools.partial(kernel, roots), out_shape=jax.ShapeDtype...]
    dot_general x15 -> x0, matrix products: 35.9 us -> none  [product(): lax.dot_general(left, right, (dims, ((), ())), precision=lax.Precision.HI...]
    unnamed x22 -> x1, local copies, waits for them, and re-layouts: 0.68 us -> 4.64 us
  transfers between devices with their start and end apart: 1 -> 0, of which waited for: 1 -> 0; matrix products, arithmetic and copies ran while one was open for 0% -> 0% of each run, Pallas kernels for 0% -> 0%
where the time goes in v2:
time: 117 us
  Pallas kernels  111 us (95%)
  local copies, waits for them, and re-layouts  4.64 us (4%)
    pallas_call x1, Pallas kernels, transform(): pl.pallas_call(functools.partial(kernel, roots), out_shape=jax.ShapeDtype...  111 us
    unnamed x1, local copies, waits for them, and re-layouts  4.64 us

profile of v2, /device:TPU:1, one launch (start us, length us, event | category | flops | bytes accessed | tf_op | source)
XLA Modules:
  0.0 116.5 jit_solution(16325910616292177404)
XLA Ops:
  0.7 111.2 %conditional.1 = (f32[2048,512]{1,0:T(8,128)}) conditional(s32[]{:T(128)} %bitcast, (f32[1,2048,256]{2,1,0:T(8,128)}, f32[2048,512]{1,0:T(8,128)}, f32[3,256,256]{2,1,0:T(8,128)}) %tuple.11, (f32[1,2048,256]{2,1,0:T(8,128)}, f32[2048,512]{1,0:T(8,128)}, f32[3,256,256]{2,1,0:T(8,128)}) %tuple.11), branch_computations={%region_0.0_spmd, %region_1.0_spmd} | conditional | bytes 8 | solution.py:397
  0.9 110.7 %transform_0.1 = f32[2048,512]{1,0:T(8,128)} custom-call(f32[1,2048,256]{2,1,0:T(8,128)} %get-tuple-element.23.slot_ref, f32[2048,512]{1,0:T(8,128)} %get-tuple-element.24.x_ref, f32[3,256,256]{2,1,0:T(8,128)} %get-tuple-element.25.t_ref), custom_call_target="tpu_custom_call" | custom-call | tf_op jit(solution)/shard_map/cond/branch_1_fun/transform_0/pallas_call | solution.py:354
  111.9 4.6 %copy.10 = f32[2048,512]{1,0:T(8,128)} copy(f32[2048,512]{1,0:T(8,128)} %get-tuple-element.26) | data formatting | bytes 8388608

commit v3 on v2

v3 whole, which is shorter than its diff:
```python
import functools

import jax
import jax.numpy as jnp
from jax import lax
from jax.experimental import pallas as pl
from jax.experimental.pallas import tpu as pltpu
from jax.sharding import PartitionSpec as P

PANELS = 3
NB = 256
SIDE = 4
TREES = 4
HOPS = 5
CHUNK = 128
LAGS = (0, 3, 6, 9, 12, 15)
UNITS = 2 * PANELS
GRID = SIDE * SIDE
DEPTH = 8
HALF = NB // 2
TILE = 512
TAIL = (
    ("a", 5), ("b", 4), ("d", 2), ("d", 3), ("f", 2), ("f", 3), ("b", 5), ("g", 0), ("g", 1), ("d", 4),
    ("g", 2), ("g", 3), ("d", 5), ("f", 4), ("g", 4), ("f", 5), ("g", 5),
)
PREP = 8
GAPS = (2, 6, 11, 12)
MESH = pl.DeviceIdType.MESH

FEED = {
    (0, 1): 0, (0, 2): 0, (0, 3): 0, (1, 0): 2, (1, 1): 2, (1, 2): 2, (1, 3): 2, (2, 0): 2,
    (2, 1): 1, (2, 2): 1, (2, 3): 2, (3, 0): 2, (3, 1): 1, (3, 2): 3, (3, 3): 3,
}
STEP = ((1, 0), (0, 1), (-1, 0), (0, -1))


def turn(node, times):
    for _ in range(times):
        node = (-node[1] % SIDE, node[0])
    return node


def build_tables():
    depth = {(0, 0): 0}

    def find(node):
        if node not in depth:
            dx, dy = STEP[FEED[node]]
            depth[node] = 1 + find(((node[0] - dx) % SIDE, (node[1] - dy) % SIDE))
        return depth[node]

    child = [[0] * 4 for _ in range(TREES)]
    deeper = [[0] * HOPS for _ in range(TREES)]
    for node in FEED:
        find(node)
        dx, dy = STEP[FEED[node]]
        parent = ((node[0] - dx) % SIDE, (node[1] - dy) % SIDE)
        for t in range(TREES):
            px, py = turn(parent, t)
            child[t][(FEED[node] + t) % 4] |= 1 << (px * SIDE + py)
            nx, ny = turn(node, t)
            for level in range(depth[node]):
                deeper[t][level] |= 1 << (nx * SIDE + ny)
    return child, deeper


CHILD, DEEPER = build_tables()


def bit(mask, place):
    return lax.rem(lax.shift_right_logical(jnp.int32(mask), place), 2)


def split(value):
    high = value.astype(jnp.bfloat16)
    return high, (value - high.astype(jnp.float32)).astype(jnp.bfloat16)


def dot(left, right, turned=False):
    dims = ((1,), (1,)) if turned else ((1,), (0,))
    return lax.dot_general(left, right, (dims, ((), ())), preferred_element_type=jnp.float32)


def dot3(left, right, turned=False):
    return dot(left[0], right[0], turned) + (dot(left[0], right[1], turned) + dot(left[1], right[0], turned))


def kernel(
    roots, slot_ref, x_ref, t_ref, state_out, panel_out, y_out,
    panel, state, xh, xl, vh, vl, acc, fromcore, chip, fromz, crossz, total, cross, yth, ytl, yh, yl,
    tree_send, tree_recv, load_sem, core_send, core_recv, z_send, z_recv, cz_send, cz_recv,
    all_send, all_recv, relay_send, relay_recv, plane_send, plane_recv, pass_send, pass_recv, out_sem,
):
    row, col = lax.axis_index("row"), lax.axis_index("col")
    x, y = col // SIDE, lax.rem(col, SIDE)
    z, core = row // 2, lax.rem(row, 2)
    near = [
        lax.rem(x + 1, SIDE) * SIDE + y,
        x * SIDE + lax.rem(y + 1, SIDE),
        lax.rem(x + 3, SIDE) * SIDE + y,
        x * SIDE + lax.rem(y + 3, SIDE),
    ]
    mate = {"row": z * 2 + 1 - core}
    rows, width = state.shape
    block = TREES * CHUNK
    count = rows // block
    half = width // 2
    slice_rows = half // DEPTH
    fill = LAGS[HOPS]

    def zplus(k):
        return lax.rem(z + k, DEPTH)

    load_x = pltpu.make_async_copy(x_ref, state, load_sem.at[2])
    load_x.start()

    barrier = pltpu.get_barrier_semaphore()
    for k in range(1, GRID):
        pl.semaphore_signal(barrier, inc=1, device_id={"col": lax.rem(col + k, GRID)}, device_id_type=MESH)
    for k in range(1, DEPTH):
        pl.semaphore_signal(barrier, inc=1, device_id={"row": zplus(k) * 2 + core}, device_id_type=MESH)
    pl.semaphore_signal(barrier, inc=1, device_id=mate, device_id_type=MESH)

    place = []
    for p in range(PANELS):
        rx, ry = roots[p] // SIDE, roots[p] % SIDE
        place.append(lax.rem(x - rx + SIDE, SIDE) * SIDE + lax.rem(y - ry + SIDE, SIDE))

        @pl.when(place[p] == 0)
        def _():
            loads = [pltpu.make_async_copy(slot_ref.at[0, :, pl.ds(h * HALF, HALF)], panel.at[p, pl.ds(h * rows, rows)], load_sem.at[h])
                     for h in range(2)]
            for load in loads:
                load.start()
            for load in loads:
                load.wait()

    zeros = jnp.zeros((32, rows), jnp.bfloat16)
    xh[width : width + 32, :] = zeros
    xl[width : width + 32, :] = zeros
    acc[...] = jnp.zeros_like(acc)
    level = [[sum(bit(m, place[p]) for m in DEEPER[t]) for t in range(TREES)] for p in range(PANELS)]
    lag = [[sum(bit(m, place[p]) * (LAGS[i + 1] - LAGS[i]) for i, m in enumerate(DEEPER[t])) + 2 * p * count
            for t in range(TREES)] for p in range(PANELS)]
    feeds = [[[bit(CHILD[t][d], place[p]) == 1 for d in range(4)] for t in range(TREES)] for p in range(PANELS)]
    fed = [place[p] != 0 for p in range(PANELS)]
    load_x.wait()
    pl.semaphore_wait(barrier, GRID - 1 + DEPTH - 1 + 1)

    def piece(p, k, t, d):
        ref = panel.at[p, pl.ds(pl.multiple_of(k * block + t * CHUNK, CHUNK), CHUNK)]
        return pltpu.make_async_remote_copy(
            src_ref=ref, dst_ref=ref, send_sem=tree_send.at[p, t, d], recv_sem=tree_recv.at[p, k, t],
            device_id={"col": near[d]}, device_id_type=MESH,
        )

    def spread(s, low, high):
        for p in range(PANELS):
            if high <= 2 * p * count or low >= 2 * (p + 1) * count + fill:
                continue
            for t in range(TREES):
                k = s - lag[p][t]

                @pl.when(jnp.logical_and(k >= 0, k < 2 * count))
                def _():
                    @pl.when(fed[p])
                    def _():
                        piece(p, k, t, 0).wait_recv()

                    for d in range(4):
                        @pl.when(feeds[p][t][d])
                        def _():
                            piece(p, k, t, d).start()

    part = rows // PREP

    def prepare(i):
        at = pl.ds(pl.multiple_of(i * part, part), part)
        high, low = split(state[at, :].T)
        xh[0:width, at] = high
        xl[0:width, at] = low

    def chosen(h):
        line = lax.broadcasted_iota(jnp.int32, (16, HALF), 0)
        line = jnp.where(line // 8 == h, lax.rem(line, 8) + 8 * col, -1)
        line = jnp.where(line == lax.broadcasted_iota(jnp.int32, (16, HALF), 1), 1.0, 0.0)
        return line.astype(jnp.bfloat16)

    def gather(u, c):
        p, h = u // 2, u % 2
        at = pl.ds(pl.multiple_of(c * block, block), block)
        high, low = split(panel[p, pl.ds(pl.multiple_of(h * rows + c * block, block), block), :])
        vh[u, at, :] = high
        vl[u, at, :] = low
        tall = width if p == 0 else width + 32
        acc[u, 0:tall, :] += dot3((xh[0:tall, at], xl[0:tall, at]), (high, low))
        if p < PANELS - 1:
            strip = slice(width + 16 * p, width + 16 * p + 16)
            pick = chosen(h)
            for store, piece_of in ((xh, high), (xl, low)):
                picked = dot(pick, piece_of, True)
                if h:
                    picked = picked + store[strip, at].astype(jnp.float32)
                store[strip, at] = picked.astype(jnp.bfloat16)

    def remote(src, dst, send, recv, device):
        return pltpu.make_async_remote_copy(
            src_ref=src, dst_ref=dst, send_sem=send, recv_sem=recv, device_id=device, device_id_type=MESH
        )

    def to_mate(u):
        copies = [remote(acc.at[u, pl.ds(pl.multiple_of((1 - core) * half, half), half)], fromcore.at[u, pl.ds(0, half)],
                         core_send.at[u, 0], core_recv.at[u, 0], mate)]
        if u > 1:
            copies.append(remote(acc.at[u, pl.ds(width, 32)], fromcore.at[u, pl.ds(half, 32)],
                                 core_send.at[u, 1], core_recv.at[u, 1], mate))
        return copies

    def z_out(u):
        copies = []
        for k in range(1, DEPTH):
            there = {"row": zplus(k) * 2 + core}
            copies.append(remote(chip.at[u, pl.ds(pl.multiple_of(zplus(k) * slice_rows, slice_rows), slice_rows)],
                                 fromz.at[u, k], z_send.at[u, k], z_recv.at[u, k], there))
            if u > 1:
                tall = 8 * (u // 2)
                copies.append(remote(chip.at[u, pl.ds(half, tall)], crossz.at[u - 2, k, pl.ds(0, tall)],
                                     cz_send.at[u, k], cz_recv.at[u, k], there))
        return copies

    def mine(u, k):
        at = core * half + zplus(DEPTH - k) * slice_rows
        return total.at[u, pl.ds(pl.multiple_of(at, slice_rows), slice_rows)]

    def all_out(u):
        return [remote(mine(u, 0), mine(u, 0), all_send.at[u, k], all_recv.at[u, k], {"row": zplus(k) * 2 + core})
                for k in range(1, DEPTH)]

    def relay_out(u, k):
        return remote(mine(u, k), mine(u, k), relay_send.at[u, k], relay_recv.at[u, k], mate)

    def plane_out(u):
        ref = cross.at[u - 2, core, col]
        return [remote(ref, ref, plane_send.at[u - 2, k], plane_recv.at[u - 2, k], {"col": lax.rem(col + k, GRID)})
                for k in range(1, GRID)]

    def pass_out(u):
        ref = cross.at[u - 2, core]
        return remote(ref, ref, pass_send.at[u - 2], pass_recv.at[u - 2], mate)

    def stage_a(u):
        for copy in to_mate(u):
            copy.start()

    def stage_b(u):
        for copy in to_mate(u):
            copy.wait_recv()
        chip[u, 0:half, :] = acc[u, pl.ds(pl.multiple_of(core * half, half), half), :] + fromcore[u, 0:half, :]
        for q in range(u // 2):
            at = pl.multiple_of(16 * q + 8 * core, 8)
            chip[u, half + 8 * q : half + 8 * q + 8, :] = (
                acc[u, pl.ds(width + at, 8), :] + fromcore[u, pl.ds(half + at, 8), :]
            )
        for copy in z_out(u):
            copy.start()

    def stage_d(u):
        for copy in z_out(u):
            copy.wait_recv()
        own = chip[u, pl.ds(pl.multiple_of(z * slice_rows, slice_rows), slice_rows), :]
        for k in range(1, DEPTH):
            own = own + fromz[u, k]
        at = pl.multiple_of(core * half + z * slice_rows, slice_rows)
        total[u, pl.ds(at, slice_rows), :] = own
        for copy in all_out(u):
            copy.start()
        relay_out(u, 0).start()
        if u > 1:
            for q in range(2):
                if q < u // 2:
                    own = chip[u, half + 8 * q : half + 8 * q + 8, :]
                    for k in range(1, DEPTH):
                        own = own + crossz[u - 2, k, 8 * q : 8 * q + 8, :]
                else:
                    own = jnp.zeros((8, HALF), jnp.float32)
                cross[u - 2, core, col, q] = own
            for copy in plane_out(u):
                copy.start()

    def stage_f(u):
        for k, copy in enumerate(all_out(u), 1):
            copy.wait_recv()
            relay_out(u, k).start()
        if u > 1:
            for copy in plane_out(u):
                copy.wait_recv()
            pass_out(u).start()

    def stage_g(u):
        for k in range(DEPTH):
            relay_out(u, k).wait_recv()
        if u > 1:
            pass_out(u).wait_recv()
        if u % 2 == 0:
            return
        p = u // 2
        inner = jnp.concatenate([total[u - 1], total[u]], axis=1)
        for q in range(p):
            mixed = jnp.concatenate([cross[u - 3, :, :, q].reshape(NB, HALF), cross[u - 2, :, :, q].reshape(NB, HALF)], axis=1)
            inner = inner - dot3((yth[q], ytl[q]), split(mixed))
        scaled = dot3(split(inner), split(t_ref[p]), True)
        if p == PANELS - 1:
            y_out[...] = scaled.T
            return
        yth[p], ytl[p] = split(scaled)
        yh[...], yl[...] = split(scaled.T)

        def update(i, carry):
            at = pl.ds(pl.multiple_of(i * 256, 256), 256)
            high = jnp.concatenate([vh[u - 1, at, :], vh[u, at, :]], axis=1)
            low = jnp.concatenate([vl[u - 1, at, :], vl[u, at, :]], axis=1)
            state[at, :] = state[at, :] - dot3((high, low), (yh[...], yl[...]))
            return carry

        lax.fori_loop(0, rows // 256, update, 0)
        if p == PANELS - 2:
            pltpu.make_async_copy(state, state_out, out_sem.at[0]).start()

    steps = UNITS * count + fill
    plan = []
    for u in range(UNITS):
        end = (u + 1) * count + fill
        for stage, gap in ((stage_a, 0), (stage_b, GAPS[0]), (stage_d, GAPS[1]), (stage_f, GAPS[2]), (stage_g, GAPS[3])):
            plan.append((end + gap, u, stage))
    plan.sort(key=lambda entry: entry[:2])
    late = [entry for entry in plan if entry[0] >= steps]
    plan = [entry for entry in plan if entry[0] < steps]
    cuts = sorted({0, PREP, fill, steps} | {fill + u * count for u in range(1, UNITS)})
    for low, high in zip(cuts, cuts[1:]):
        def turn_step(s, carry):
            for step, u, stage in plan:
                if low <= step < high:
                    pl.when(s == step)(functools.partial(stage, u))
            spread(s, low, high)
            if low < PREP:
                prepare(s)
            if low >= fill:
                u = (low - fill) // count
                gather(u, s - fill - u * count)
            return carry

        lax.fori_loop(low, high, turn_step, 0)

    last = pltpu.make_async_copy(panel.at[PANELS - 1], panel_out, out_sem.at[1])
    last.start()
    pending = {(stage, u) for _, u, stage in late}
    for name, u in TAIL:
        stage = {"a": stage_a, "b": stage_b, "d": stage_d, "f": stage_f, "g": stage_g}[name]
        if (stage, u) in pending:
            stage(u)

    for p in range(PANELS):
        for t in range(TREES):
            for d in range(4):
                @pl.when(feeds[p][t][d])
                def _():
                    whole = panel.at[p, pl.ds(0, 2 * rows // TREES)]
                    remote(whole, whole, tree_send.at[p, t, d], tree_recv.at[p, 0, t], {"col": near[d]}).wait_send()
    for u in range(UNITS):
        for copy in to_mate(u) + z_out(u) + all_out(u) + [relay_out(u, k) for k in range(DEPTH)]:
            copy.wait_send()
        if u > 1:
            for copy in plane_out(u) + [pass_out(u)]:
                copy.wait_send()
    pltpu.make_async_copy(state, state_out, out_sem.at[0]).wait()
    last.wait()


def transform(roots, key, slot, eigvec, tfac):
    rows, width = eigvec.shape
    count = rows // (TREES * CHUNK)
    f32, bf16 = jnp.float32, jnp.bfloat16
    dma = pltpu.SemaphoreType.DMA
    anywhere = pl.BlockSpec(memory_space=pl.ANY)
    return pl.pallas_call(
        functools.partial(kernel, roots),
        out_shape=(
            jax.ShapeDtypeStruct((rows, width), f32),
            jax.ShapeDtypeStruct((2 * rows, HALF), f32),
            jax.ShapeDtypeStruct((NB, width), f32),
        ),
        in_specs=[anywhere, anywhere, pl.BlockSpec(memory_space=pltpu.VMEM)],
        out_specs=(anywhere, anywhere, pl.BlockSpec(memory_space=pltpu.VMEM)),
        scratch_shapes=[
            pltpu.VMEM((PANELS, 2 * rows, HALF), f32),
            pltpu.VMEM((rows, width), f32),
            pltpu.VMEM((width + 32, rows), bf16),
            pltpu.VMEM((width + 32, rows), bf16),
            pltpu.VMEM((UNITS, rows, HALF), bf16),
            pltpu.VMEM((UNITS, rows, HALF), bf16),
            pltpu.VMEM((UNITS, width + 32, HALF), f32),
            pltpu.VMEM((UNITS, width // 2 + 32, HALF), f32),
            pltpu.VMEM((UNITS, width // 2 + 16, HALF), f32),
            pltpu.VMEM((UNITS, DEPTH, width // 2 // DEPTH, HALF), f32),
            pltpu.VMEM((UNITS - 2, DEPTH, 16, HALF), f32),
            pltpu.VMEM((UNITS, width, HALF), f32),
            pltpu.VMEM((UNITS - 2, 2, GRID, 2, 8, HALF), f32),
            pltpu.VMEM((PANELS - 1, width, NB), bf16),
            pltpu.VMEM((PANELS - 1, width, NB), bf16),
            pltpu.VMEM((NB, width), bf16),
            pltpu.VMEM((NB, width), bf16),
            dma((PANELS, TREES, 4)),
            dma((PANELS, 2 * count, TREES)),
            dma((3,)),
            dma((UNITS, 2)), dma((UNITS, 2)),
            dma((UNITS, DEPTH)), dma((UNITS, DEPTH)),
            dma((UNITS, DEPTH)), dma((UNITS, DEPTH)),
            dma((UNITS, DEPTH)), dma((UNITS, DEPTH)),
            dma((UNITS, DEPTH)), dma((UNITS, DEPTH)),
            dma((UNITS - 2, GRID)), dma((UNITS - 2, GRID)),
            dma((UNITS - 2,)), dma((UNITS - 2,)),
            dma((2,)),
        ],
        compiler_params=pltpu.CompilerParams(
            collective_id=key, has_side_effects=True, vmem_limit_bytes=58 << 20
        ),
        name="transform_%d" % key,
    )(slot, eigvec, tfac)


def finish_kernel(state_ref, left_ref, right_ref, y_ref, out_ref, yh, yl):
    @pl.when(pl.program_id(0) == 0)
    def _():
        yh[...], yl[...] = split(y_ref[...])

    piece = split(jnp.concatenate([left_ref[...], right_ref[...]], axis=1))
    out_ref[...] = state_ref[...] - dot3(piece, (yh[...], yl[...]))


def finish(state, panel, scaled):
    rows, width = state.shape
    return pl.pallas_call(
        finish_kernel,
        out_shape=jax.ShapeDtypeStruct((rows, width), jnp.float32),
        grid=(rows // TILE,),
        in_specs=[
            pl.BlockSpec((TILE, width), lambda i: (i, 0)),
            pl.BlockSpec((TILE, HALF), lambda i: (i, 0)),
            pl.BlockSpec((TILE, HALF), lambda i: (i + rows // TILE, 0)),
            pl.BlockSpec((NB, width), lambda i: (0, 0)),
        ],
        out_specs=pl.BlockSpec((TILE, width), lambda i: (i, 0)),
        scratch_shapes=[pltpu.VMEM((NB, width), jnp.bfloat16), pltpu.VMEM((NB, width), jnp.bfloat16)],
        name="finish",
    )(state, panel, panel, scaled)


def shards(eigvec, slots, roots, tfac):
    state, panel, scaled = lax.cond(
        roots[0] == GRID - 2,
        functools.partial(transform, (GRID - 2, GRID - 1, 0), 0),
        functools.partial(transform, (GRID - 1, 0, 1), 1),
        slots, eigvec, tfac,
    )
    return finish(state, panel, scaled)


def solution(mesh):
    in_specs = (P("row", "col"), P("col", "row", None), P(), P())
    out_specs = P("row", "col")
    return jax.shard_map(shards, mesh=mesh, in_specs=in_specs, out_specs=out_specs, check_vma=False)
```

time: 117 us -> 117 us (level)
  Pallas kernels: 111 us -> 116 us
  local copies, waits for them, and re-layouts: 4.64 us -> 0 us
    pallas_call x1 -> x2, Pallas kernels: 111 us -> 116 us  [the longest x1 110 us: transform(): pl.pallas_call(functools.partial(kernel, roots), out_shape=(jax.ShapeDtyp...]
    unnamed x1 -> x0, local copies, waits for them, and re-layouts: 4.64 us -> none
where the time goes in v3:
time: 117 us
  Pallas kernels  116 us (99%)
    pallas_call x1, Pallas kernels, transform(): pl.pallas_call(functools.partial(kernel, roots), out_shape=(jax.ShapeDtyp...  110 us
    pallas_call x1, Pallas kernels, finish(): pl.pallas_call(finish_kernel, out_shape=jax.ShapeDtypeStruct((rows, width...  5.89 us

profile of v3, /device:TPU:1, one launch (start us, length us, event | category | flops | bytes accessed | tf_op | source)
XLA Modules:
  0.0 116.5 jit_solution(4426073910000772411)
XLA Ops:
  0.7 110.0 %conditional.1 = ((f32[2048,512]{1,0:T(8,128)}, f32[4096,128]{1,0:T(8,128)S(1)}, f32[256,512]{1,0:T(8,128)S(1)})) conditional(s32[]{:T(128)} %bitcast, (f32[1,2048,256]{2,1,0:T(8,128)}, f32[2048,512]{1,0:T(8,128)}, f32[3,256,256]{2,1,0:T(8,128)}) %tuple.11, (f32[1,2048,256]{2,1,0:T(8,128)}, f32[2048,512]{1,0:T(8,128)}, f32[3,256,256]{2,1,0:T(8,128)}) %tuple.11), branch_computations={%region_0.0_spmd, %region_1.0_spmd} | conditional | bytes 8 | solution.py:459
  0.9 109.8 %transform_0.1 = (f32[2048,512]{1,0:T(8,128)}, f32[4096,128]{1,0:T(8,128)S(1)}, f32[256,512]{1,0:T(8,128)S(1)}) custom-call(f32[1,2048,256]{2,1,0:T(8,128)} %get-tuple-element.20.slot_ref, f32[2048,512]{1,0:T(8,128)} %get-tuple-element.21.x_ref, f32[3,256,256]{2,1,0:T(8,128)} %get-tuple-element.22.t_ref), custom_call_target="tpu_custom_call" | custom-call | tf_op jit(solution)/shard_map/cond/branch_1_fun/transform_0/pallas_call | solution.py:385
  110.6 5.9 %finish.1 = f32[2048,512]{1,0:T(8,128)} custom-call(f32[2048,512]{1,0:T(8,128)} %get-tuple-element.26.state_ref, f32[4096,128]{1,0:T(8,128)S(1)} %get-tuple-element.27.left_ref.right_ref, f32[4096,128]{1,0:T(8,128)S(1)} %get-tuple-element.27.left_ref.right_ref, f32[256,512]{1,0:T(8,128)S(1)} %get-tuple-element.28.y_ref), custom_call_target="tpu_custom_call" | custom-call | tf_op jit(solution)/shard_map/finish/pallas_call | solution.py:442

commit v4 on v3

--- a/solution.py
+++ b/solution.py
@@ -20,7 +20,7 @@
 HALF = NB // 2
 TILE = 512
 TAIL = (
-    ("a", 5), ("b", 4), ("d", 2), ("d", 3), ("f", 2), ("f", 3), ("b", 5), ("g", 0), ("g", 1), ("d", 4),
+    ("a", 5), ("b", 4), ("d", 2), ("d", 3), ("b", 5), ("f", 2), ("f", 3), ("g", 0), ("g", 1), ("d", 4),
     ("g", 2), ("g", 3), ("d", 5), ("f", 4), ("g", 4), ("f", 5), ("g", 5),
 )
 PREP = 8

time: 117 us -> 117 us (level); the launches traced: 117 us -> 115 us
  Pallas kernels: 116 us -> 114 us
    pallas_call x1, Pallas kernels: 110 us -> 108 us  [transform(): pl.pallas_call(functools.partial(kernel, roots), out_shape=(jax.ShapeDtyp...]
where the time goes in v4:
time: 117 us; the launch traced here: 115 us
  Pallas kernels  114 us (97%)
    pallas_call x1, Pallas kernels, transform(): pl.pallas_call(functools.partial(kernel, roots), out_shape=(jax.ShapeDtyp...  108 us
    pallas_call x1, Pallas kernels, finish(): pl.pallas_call(finish_kernel, out_shape=jax.ShapeDtypeStruct((rows, width...  5.88 us

profile of v4, /device:TPU:1, one launch (start us, length us, event | category | flops | bytes accessed | tf_op | source)
XLA Modules:
  0.0 115.2 jit_solution(8349112777374330480)
XLA Ops:
  0.7 108.6 %conditional.1 = ((f32[2048,512]{1,0:T(8,128)}, f32[4096,128]{1,0:T(8,128)S(1)}, f32[256,512]{1,0:T(8,128)S(1)})) conditional(s32[]{:T(128)} %bitcast, (f32[1,2048,256]{2,1,0:T(8,128)}, f32[2048,512]{1,0:T(8,128)}, f32[3,256,256]{2,1,0:T(8,128)}) %tuple.11, (f32[1,2048,256]{2,1,0:T(8,128)}, f32[2048,512]{1,0:T(8,128)}, f32[3,256,256]{2,1,0:T(8,128)}) %tuple.11), branch_computations={%region_0.0_spmd, %region_1.0_spmd} | conditional | bytes 8 | solution.py:459
  0.9 108.4 %transform_0.1 = (f32[2048,512]{1,0:T(8,128)}, f32[4096,128]{1,0:T(8,128)S(1)}, f32[256,512]{1,0:T(8,128)S(1)}) custom-call(f32[1,2048,256]{2,1,0:T(8,128)} %get-tuple-element.20.slot_ref, f32[2048,512]{1,0:T(8,128)} %get-tuple-element.21.x_ref, f32[3,256,256]{2,1,0:T(8,128)} %get-tuple-element.22.t_ref), custom_call_target="tpu_custom_call" | custom-call | tf_op jit(solution)/shard_map/cond/branch_1_fun/transform_0/pallas_call | solution.py:385
  109.3 5.9 %finish.1 = f32[2048,512]{1,0:T(8,128)} custom-call(f32[2048,512]{1,0:T(8,128)} %get-tuple-element.26.state_ref, f32[4096,128]{1,0:T(8,128)S(1)} %get-tuple-element.27.left_ref.right_ref, f32[4096,128]{1,0:T(8,128)S(1)} %get-tuple-element.27.left_ref.right_ref, f32[256,512]{1,0:T(8,128)S(1)} %get-tuple-element.28.y_ref), custom_call_target="tpu_custom_call" | custom-call | tf_op jit(solution)/shard_map/finish/pallas_call | solution.py:442
